TPU v7x, 128 devices: a whole 4x4x4 slice. The times are simulated.
128 devices in a mesh: brick: 8 (over y, core), grp: 16 (over x, z).
Axes of the slice: x: 4, y: 4, z: 4, core: 2. Of those that a mesh axis runs over, the one named last changes fastest.
Arguments:
- source: float32 [16, 8, 2, 32, 1024], P('grp', 'brick'), may hold values from -21 to 21
- uptake: float32 [16, 8, 2, 32, 1024], P('grp', 'brick'), may hold values from 0.00015 to 0.006
- conductance: float32 [16, 8, 6, 2, 32, 1024], P('grp', 'brick'), may hold values from 0 to 3, as said below
- occupancy: int32 [16, 2, 8], replicated, may hold values from 0 to 1, as said below
- assignment: int32 [8], replicated, may hold values from 0 to 7, as said below
Outputs:
- solution_field: float32 [16, 8, 2, 32, 1024], P('grp', 'brick')
- residual: float32 [16, 8, 2, 32, 1024], P('grp', 'brick')
Inputs may be any that keep to these rules, and one draw needn't show every extreme that they name: `occupancy`: 1 marks an occupied brick; in every draw one patch of some slab has all its bricks occupied. `assignment`: each patch is held by exactly one index of brick. `conductance`: equal at both ends of a bond: the value toward +x at a cell is the value toward -x at its +x neighbour, likewise for y and z, the lattice being read cyclically; values toward +z and -z are 0.3 or more.
All inputs are finite; a program needn't handle non-finite values.
Results may differ from a plain program's by a relative error of at most 0.0003.
Values sent between devices are 32-bit elements; how exact they have to be, the bound alone decides.
A program may use at most 128 MiB of HBM per device.

v0:
```python
import jax
import jax.numpy as jnp
from jax import lax
from jax.sharding import PartitionSpec as P

BS = 32
PATCH_X = 1
PATCH_Y = 2
ITERS = 3
OMEGA = 0.6


def extended_2(block, sides, width):
    for axis, dim in sides:
        count = lax.axis_size(axis)
        forward = [(i, i + 1) for i in range(count - 1)]
        backward = [(target, source) for source, target in forward]
        low = lax.ppermute(
            lax.slice_in_dim(block, block.shape[dim] - width, None, axis=dim), axis, forward
        )
        high = lax.ppermute(lax.slice_in_dim(block, 0, width, axis=dim), axis, backward)
        block = jnp.concatenate([low, block, high], axis=dim)
    return block


def assemble(coarse_diag, couplings, strides):
    extent = coarse_diag.shape[0]
    matrix = jnp.diag(coarse_diag)
    for coupling, stride in zip(couplings, strides):
        banded = coupling[: extent - stride]
        matrix = matrix - jnp.diag(banded, stride) - jnp.diag(banded, -stride)
    return matrix


def pad_rows(block, capacity):
    return jnp.pad(block, ((0, capacity - block.shape[0]), (0, 0)))


def on_device(source, uptake, conductance, occupancy, assignment):
    face_size = BS * BS
    capacity = max(PATCH_X, PATCH_Y)
    slot_count = PATCH_X * PATCH_Y
    slab_index = lax.axis_index("grp")
    brick_index = lax.axis_index("brick")
    brick_count = lax.axis_size("brick")
    across = brick_count // 2
    peer_ids = jnp.arange(brick_count, dtype=jnp.int32)
    patch_index = assignment[brick_index]
    patch_row = patch_index // across
    patch_column = patch_index % across

    def owner_of(row_shift, column_shift):
        row_target = patch_row + row_shift
        column_target = patch_column + column_shift
        inside = (
            (row_target >= 0) & (row_target < 2) & (column_target >= 0) & (column_target < across)
        )
        holder = jnp.sum(jnp.where(assignment == row_target * across + column_target, peer_ids, 0))
        return jnp.where(inside, holder, -1)

    wanted = jnp.stack([owner_of(1, 0), owner_of(-1, 0), owner_of(0, 1), owner_of(0, -1)])
    padded = jnp.pad(occupancy, 1)
    window = lax.dynamic_slice(
        padded,
        (slab_index, patch_row * PATCH_X, patch_column * PATCH_Y),
        (3, PATCH_X + 2, PATCH_Y + 2),
    ).astype(jnp.float32)
    centre = window[1, 1:-1, 1:-1].reshape(slot_count)
    toward = [
        window[1, 2:, 1:-1],
        window[1, :-2, 1:-1],
        window[1, 1:-1, 2:],
        window[1, 1:-1, :-2],
        window[2, 1:-1, 1:-1],
        window[0, 1:-1, 1:-1],
    ]
    first_axis = lax.broadcasted_iota(jnp.int32, (1, BS, face_size), 1)
    flat_axis = lax.broadcasted_iota(jnp.int32, (1, BS, face_size), 2)
    second_axis = flat_axis // BS
    third_axis = flat_axis % BS
    cube_third = lax.broadcasted_iota(jnp.int32, (1, BS, BS, BS), 3)
    borders = [
        first_axis == BS - 1,
        first_axis == 0,
        second_axis == BS - 1,
        second_axis == 0,
        third_axis == BS - 1,
        third_axis == 0,
    ]
    bonds = conductance[0, 0]
    live_here = centre[:, None, None]
    effective = []
    for direction in range(6):
        neighbour_live = toward[direction].reshape(slot_count)[:, None, None]
        active = jnp.where(borders[direction], live_here * neighbour_live, live_here)
        effective.append(bonds[direction] * active)
    absorb = uptake[0, 0]
    diagonal = absorb
    for direction in range(6):
        diagonal = diagonal + effective[direction]

    def apply_operator(field):
        lower_x = field[:, 0, :]
        upper_x = field[:, BS - 1, :]
        lower_y = field[:, :, :BS].reshape(slot_count, face_size)
        upper_y = field[:, :, face_size - BS :].reshape(slot_count, face_size)
        cube = field.reshape(slot_count, BS, BS, BS)
        lower_z = cube[:, :, :, 0].reshape(slot_count, face_size)
        upper_z = cube[:, :, :, BS - 1].reshape(slot_count, face_size)
        grid_lower_x = lower_x.reshape(PATCH_X, PATCH_Y, face_size)
        grid_upper_x = upper_x.reshape(PATCH_X, PATCH_Y, face_size)
        grid_lower_y = lower_y.reshape(PATCH_X, PATCH_Y, face_size)
        grid_upper_y = upper_y.reshape(PATCH_X, PATCH_Y, face_size)
        outgoing_sides = jnp.stack(
            [
                pad_rows(grid_lower_x[0], capacity),
                pad_rows(grid_upper_x[PATCH_X - 1], capacity),
                pad_rows(grid_lower_y[:, 0], capacity),
                pad_rows(grid_upper_y[:, PATCH_Y - 1], capacity),
            ]
        )
        portion = lax.all_gather(outgoing_sides[None], "brick", axis=0, tiled=True)
        sources = jnp.arange(portion.shape[0], dtype=jnp.int32)
        matches = sources[:, None] == wanted[None, :]
        remote = jnp.zeros((4, capacity, face_size), jnp.float32) + jnp.sum(
            jnp.where(matches[:, :, None, None], portion, 0.0), axis=0
        )
        stacked = jnp.stack([lower_z, upper_z])
        extended = extended_2(stacked, (("grp", 0),), 1)
        from_below = extended[0].reshape(slot_count, BS, BS, 1)
        from_above = extended[3].reshape(slot_count, BS, BS, 1)
        beyond_xplus = jnp.concatenate(
            [grid_lower_x[1:], remote[0, :PATCH_Y][None]], axis=0
        ).reshape(slot_count, face_size)
        beyond_xminus = jnp.concatenate(
            [remote[1, :PATCH_Y][None], grid_upper_x[:-1]], axis=0
        ).reshape(slot_count, face_size)
        beyond_yplus = jnp.concatenate(
            [grid_lower_y[:, 1:], remote[2, :PATCH_X][:, None]], axis=1
        ).reshape(slot_count, BS, BS)
        beyond_yminus = jnp.concatenate(
            [remote[3, :PATCH_X][:, None], grid_upper_y[:, :-1]], axis=1
        ).reshape(slot_count, BS, BS)
        upper_neighbour = jnp.where(
            cube_third == BS - 1, from_above, jnp.roll(cube, -1, axis=3)
        ).reshape(slot_count, BS, face_size)
        lower_neighbour = jnp.where(cube_third == 0, from_below, jnp.roll(cube, 1, axis=3)).reshape(
            slot_count, BS, face_size
        )
        total = diagonal * field
        total = total - effective[0] * jnp.concatenate(
            [field[:, 1:, :], beyond_xplus[:, None, :]], axis=1
        )
        total = total - effective[1] * jnp.concatenate(
            [beyond_xminus[:, None, :], field[:, :-1, :]], axis=1
        )
        total = total - effective[2] * jnp.concatenate([field[:, :, BS:], beyond_yplus], axis=2)
        total = total - effective[3] * jnp.concatenate(
            [beyond_yminus, field[:, :, : face_size - BS]], axis=2
        )
        total = total - effective[4] * upper_neighbour
        total = total - effective[5] * lower_neighbour
        return total

    slot_ids = jnp.arange(slot_count)
    brick_first = slot_ids // PATCH_Y
    brick_second = slot_ids % PATCH_Y
    inside = [
        (brick_first < PATCH_X - 1).astype(jnp.float32),
        (brick_first > 0).astype(jnp.float32),
        (brick_second < PATCH_Y - 1).astype(jnp.float32),
        (brick_second > 0).astype(jnp.float32),
    ]
    face_sums = [
        jnp.sum(effective[0][:, BS - 1, :], axis=1),
        jnp.sum(effective[1][:, 0, :], axis=1),
        jnp.sum(effective[2][:, :, face_size - BS :], axis=(1, 2)),
        jnp.sum(effective[3][:, :, :BS], axis=(1, 2)),
        jnp.sum(effective[4].reshape(slot_count, BS, BS, BS)[:, :, :, BS - 1], axis=(1, 2)),
        jnp.sum(effective[5].reshape(slot_count, BS, BS, BS)[:, :, :, 0], axis=(1, 2)),
    ]
    coarse_diag = jnp.sum(absorb, axis=(1, 2))
    for direction in range(4):
        coarse_diag = coarse_diag + face_sums[direction] * inside[direction]
    coarse_diag = coarse_diag + face_sums[4] + face_sums[5]
    record = jnp.stack(
        [coarse_diag, face_sums[0] * inside[0], face_sums[2] * inside[2], face_sums[4]]
    )[None]
    gathered = lax.all_gather(record, "grp", axis=0, tiled=True)
    columns = jnp.transpose(gathered, (1, 0, 2)).reshape(4, -1)
    matrix = assemble(columns[0], (columns[1], columns[2], columns[3]), (PATCH_Y, 1, slot_count))
    factor = jnp.linalg.cholesky(matrix)

    def coarse_solve(residual_field):
        totals = jnp.sum(residual_field, axis=(1, 2))
        gathered_terms = lax.all_gather(totals[None], "grp", axis=0, tiled=True).reshape(-1, 1)
        middle = lax.linalg.triangular_solve(factor, gathered_terms, left_side=True, lower=True)
        result = lax.linalg.triangular_solve(
            factor, middle, left_side=True, lower=True, transpose_a=True
        )
        return lax.dynamic_slice_in_dim(result[:, 0], slab_index * slot_count, slot_count)

    def precondition(residual_field):
        smoothed = OMEGA * residual_field / diagonal
        smoothed = smoothed + OMEGA * (residual_field - apply_operator(smoothed)) / diagonal
        return smoothed + coarse_solve(residual_field)[:, None, None]

    forcing = source[0, 0] * live_here
    solution_field = jnp.zeros_like(forcing)
    residual = forcing

    def global_sum(values):
        return lax.psum(jnp.sum(values), ("brick", "grp"))

    search = precondition(residual)
    energy = global_sum(residual * search)
    for iteration in range(ITERS):
        mapped = apply_operator(search)
        step_size = energy / global_sum(search * mapped)
        solution_field = solution_field + step_size * search
        residual = residual - step_size * mapped
        if iteration + 1 < ITERS:
            smoothed = precondition(residual)
            renewed = global_sum(residual * smoothed)
            search = smoothed + renewed / energy * search
            energy = renewed
    return (solution_field[None, None], residual[None, None])


def solution(mesh):
    return jax.shard_map(
        on_device,
        mesh=mesh,
        in_specs=(
            P("grp", "brick", None, None, None),
            P("grp", "brick", None, None, None),
            P("grp", "brick", None, None, None, None),
            P(),
            P(),
        ),
        out_specs=(P("grp", "brick", None, None, None), P("grp", "brick", None, None, None)),
        check_vma=False,
    )
```

profile of v0, /device:TPU:1, one launch (start us, length us, event | category | flops | bytes accessed | tf_op | source)
XLA Modules:
  0.0 1063.9 jit_solution(14409875242148923339)
XLA Ops:
  15.4 2.4 squeeze.120
  22.2 5.7 multiply_divide_fusion.2
  30.5 4.9 collective-permute-start.1
  45.7 14.1 %all-gather = f32[32,2,1024]{2,1,0:T(2,128)S(1)} all-gather(f32[4,2,1024]{2,1,0:T(2,128)S(1)} %copy.294), channel_id=2, replica_groups=mesh['brick'=8,'grp'=16] {'brick'}, dimensions={0}, use_global_device_ids=true | all-gather | bytes 294912 | tf_op jit(solution)/shard_map/all_gather | solution.py:122
  68.6 19.9 %all-gather.10 = f32[16,4,2]{1,2,0:T(2,128)S(1)} all-gather(f32[1,4,2]{1,2,0:T(2,128)S(1)} %bitcast.616), channel_id=3, replica_groups=mesh['brick'=8,'grp'=16] {'grp'}, dimensions={0}, use_global_device_ids=true | all-gather | bytes 544 | tf_op jit(solution)/shard_map/all_gather | solution.py:189
  94.2 31.1 %all-reduce.18 = f32[32]{0:T(128)S(1)} all-reduce(f32[32]{0:T(128)S(1)} %dynamic-update-slice.3), channel_id=4, replica_groups=mesh['brick'=8,'grp'=16] {'grp'}, use_global_device_ids=true, to_apply=%add.18 | all-reduce | flops 32 | bytes 256 | tf_op jit(solution)/shard_map/triangular_solve/reshape.87 | solution.py:197
  130.3 2.9 cholesky.19
  134.6 2.4 custom-call.14
  153.2 8.4 fusion.46
  167.8 2.4 broadcast_in_dim.696
  171.5 2.4 broadcast_in_dim.702
  184.6 25.6 %all-gather.3 = f32[32,2,1024]{2,1,0:T(2,128)S(1)} all-gather(f32[4,2,1024]{2,1,0:T(2,128)S(1)} %copy.298), channel_id=5, replica_groups=mesh['brick'=8,'grp'=16] {'brick'}, dimensions={0}, use_global_device_ids=true | all-gather | bytes 294912 | tf_op jit(solution)/shard_map/all_gather | solution.py:122
  226.1 3.0 pad_maximum_fusion.2
  231.1 2.4 concatenate.676
  233.6 2.4 concatenate.677
  282.5 3.7 multiply_reduce_fusion.3
  286.2 64.0 %all-reduce.21 = (f32[]{:T(128)}, f32[]{:T(128)}) all-reduce(f32[]{:T(128)} %get-tuple-element.21, f32[]{:T(128)} %get-tuple-element.20), channel_id=1, replica_groups=mesh['brick'=8,'grp'=16] {'brick','grp'}, use_global_device_ids=true, to_apply=%region_16.19 | all-reduce | flops 2 | bytes 16 | tf_op jit(solution)/shard_map/psum | solution.py:213
  362.0 13.5 %all-gather.4 = f32[32,2,1024]{2,1,0:T(2,128)S(1)} all-gather(f32[4,2,1024]{2,1,0:T(2,128)S(1)} %copy.304), channel_id=6, replica_groups=mesh['brick'=8,'grp'=16] {'brick'}, dimensions={0}, use_global_device_ids=true | all-gather | bytes 294912 | tf_op jit(solution)/shard_map/all_gather | solution.py:122
  385.3 9.1 multiply_divide_fusion.1
  400.2 31.6 %all-reduce.19 = f32[32]{0:T(128)} all-reduce(f32[32]{0:T(128)} %dynamic-update-slice.4), channel_id=7, replica_groups=mesh['brick'=8,'grp'=16] {'grp'}, use_global_device_ids=true, to_apply=%add.19 | all-reduce | flops 32 | bytes 256 | tf_op jit(solution)/shard_map/triangular_solve/reshape.87 | solution.py:197
  442.0 3.0 pad_maximum_fusion.4
  447.3 3.0 fusion.96
  487.2 3.7 multiply_reduce_fusion.2
  490.9 71.1 %psum.44 = f32[]{:T(128)} all-reduce(f32[]{:T(128)} %get-tuple-element.54), channel_id=1, replica_groups=mesh['brick'=8,'grp'=16] {'brick','grp'}, use_global_device_ids=true, to_apply=%region_23.26 | all-reduce | flops 1 | bytes 8 | tf_op jit(solution)/shard_map/psum | solution.py:213
  565.9 13.6 %all-gather.6 = f32[32,2,1024]{2,1,0:T(2,128)S(1)} all-gather(f32[4,2,1024]{2,1,0:T(2,128)S(1)} %copy.309), channel_id=8, replica_groups=mesh['brick'=8,'grp'=16] {'brick'}, dimensions={0}, use_global_device_ids=true | all-gather | bytes 294912 | tf_op jit(solution)/shard_map/all_gather | solution.py:122
  588.0 7.3 multiply_add_fusion.1
  603.4 2.7 pad_maximum_fusion.6
  607.5 2.5 broadcast_in_dim.764
  620.1 2.5 concatenate.791
  630.3 2.5 broadcast_in_dim.760
  637.4 3.3 multiply_reduce_fusion.1
  640.7 66.1 %psum.45 = f32[]{:T(128)} all-reduce(f32[]{:T(128)} %get-tuple-element.50), channel_id=1, replica_groups=mesh['brick'=8,'grp'=16] {'brick','grp'}, use_global_device_ids=true, to_apply=%region_26.29 | all-reduce | flops 1 | bytes 8 | tf_op jit(solution)/shard_map/psum | solution.py:213
  711.4 13.5 %all-gather.7 = f32[32,2,1024]{2,1,0:T(2,128)S(1)} all-gather(f32[4,2,1024]{2,1,0:T(2,128)S(1)} %copy.314), channel_id=9, replica_groups=mesh['brick'=8,'grp'=16] {'brick'}, dimensions={0}, use_global_device_ids=true | all-gather | bytes 294912 | tf_op jit(solution)/shard_map/all_gather | solution.py:122
  733.8 8.2 multiply_divide_fusion
  747.8 31.5 %all-reduce.20 = f32[32]{0:T(128)} all-reduce(f32[32]{0:T(128)} %dynamic-update-slice.5), channel_id=10, replica_groups=mesh['brick'=8,'grp'=16] {'grp'}, use_global_device_ids=true, to_apply=%add.20 | all-reduce | flops 32 | bytes 256 | tf_op jit(solution)/shard_map/triangular_solve/reshape.87 | solution.py:197
  788.1 3.0 pad_maximum_fusion.8
  823.6 2.4 broadcast_in_dim.771
  831.9 3.8 multiply_reduce_fusion
  835.8 70.9 %psum.46 = f32[]{:T(128)} all-reduce(f32[]{:T(128)} %get-tuple-element.42), channel_id=1, replica_groups=mesh['brick'=8,'grp'=16] {'brick','grp'}, use_global_device_ids=true, to_apply=%region_30.33 | all-reduce | flops 1 | bytes 8 | tf_op jit(solution)/shard_map/psum | solution.py:213
  914.6 13.8 %all-gather.9 = f32[32,2,1024]{2,1,0:T(2,128)S(1)} all-gather(f32[4,2,1024]{2,1,0:T(2,128)S(1)} %copy.319), channel_id=11, replica_groups=mesh['brick'=8,'grp'=16] {'brick'}, dimensions={0}, use_global_device_ids=true | all-gather | bytes 294912 | tf_op jit(solution)/shard_map/all_gather | solution.py:122
  938.2 10.7 %multiply_add_fusion = f32[2,32,32,32]{3,2,1,0:T(8,128)S(1)} fusion(f32[2,32,32,32]{3,2,1,0:T(8,128)} %copy-done.5, f32[2,32,32,32]{3,2,1,0:T(8,128)} %get-tuple-element.75, f32[2,32,32,32]{3,2,1,0:T(8,128)} %get-tuple-element.77, f32[2,32,32,32]{3,2,1,0:T(8,128)} %get-tuple-element.76, f32[2,32,32,32]{3,2,1,0:T(8,128)} %concatenate.773, ...), kind=kLoop, calls=%fused_computation.76 | loop fusion | flops 3735552 | bytes 5865592 | tf_op jit(solution)/shard_map/add | solution.py:225
  959.3 2.4 broadcast_in_dim.783
  966.9 2.4 concatenate.818
  969.3 2.4 concatenate.775
  978.0 2.5 broadcast_in_dim.779
  984.3 2.6 fusion.155
  988.6 66.6 %psum.47 = f32[]{:T(128)} all-reduce(f32[]{:T(128)} %fusion.155), channel_id=1, replica_groups=mesh['brick'=8,'grp'=16] {'brick','grp'}, use_global_device_ids=true, to_apply=%region_33.36 | all-reduce | flops 1 | bytes 8 | tf_op jit(solution)/shard_map/psum | solution.py:213
  1056.6 6.0 fusion.149
  (713 shorter events, 371.7 us)
Async XLA Ops:
  0.6 9.8 copy-start.37
  0.6 11.2 %copy-start = (f32[1,1,6,2,32,1024]{5,4,3,2,1,0:T(8,128)S(1)}, f32[1,1,6,2,32,1024]{5,4,3,2,1,0:T(8,128)}, u32[]{:S(2)}) copy-start(f32[1,1,6,2,32,1024]{5,4,3,2,1,0:T(8,128)} %param.11) | copy-start | bytes 4718596
  4.7 34.9 %copy-start.95 = (pred[32]{0:T(512)(128)(4,1)}, pred[32]{0:T(512)(128)(4,1)S(1)}, u32[]{:S(2)}) copy-start(pred[32]{0:T(512)(128)(4,1)S(1)} %get-tuple-element.277) | copy-start | bytes 100
  4.7 34.9 %copy-start.101 = (pred[32]{0:T(512)(128)(4,1)}, pred[32]{0:T(512)(128)(4,1)S(1)}, u32[]{:S(2)}) copy-start(pred[32]{0:T(512)(128)(4,1)S(1)} %get-tuple-element.278) | copy-start | bytes 100
  8.2 31.4 %copy-start.85 = (f32[2]{0:T(128)}, f32[2]{0:T(128)S(1)}, u32[]{:S(2)}) copy-start(f32[2]{0:T(128)S(1)} %get-tuple-element.32) | copy-start | bytes 28
  22.2 17.4 %copy-start.118 = (f32[2]{0:T(128)}, f32[2]{0:T(128)S(1)}, u32[]{:S(2)}) copy-start(f32[2]{0:T(128)S(1)} %get-tuple-element.268) | copy-start | bytes 28
  27.9 10.7 %copy-start.20 = (f32[1,1,2,32,1024]{4,3,2,1,0:T(8,128)S(1)}, f32[1,1,2,32,1024]{4,3,2,1,0:T(8,128)}, u32[]{:S(2)}) copy-start(f32[1,1,2,32,1024]{4,3,2,1,0:T(8,128)} %param.9) | copy-start | bytes 786436
  28.0 11.6 %copy-start.38 = (f32[1,1,2,32,1024]{4,3,2,1,0:T(8,128)S(1)}, f32[1,1,2,32,1024]{4,3,2,1,0:T(8,128)}, u32[]{:S(2)}) copy-start(f32[1,1,2,32,1024]{4,3,2,1,0:T(8,128)} %param.10) | copy-start | bytes 786436
  28.0 11.6 %copy-start.122 = (f32[2]{0:T(128)S(1)}, f32[2]{0:T(128)}, u32[]{:S(2)}) copy-start(f32[2]{0:T(128)} %copy-done.121) | copy-start | bytes 28
  28.0 11.6 %copy-start.125 = (f32[2]{0:T(128)S(1)}, f32[2]{0:T(128)}, u32[]{:S(2)}) copy-start(f32[2]{0:T(128)} %copy-done.124) | copy-start | bytes 28
  28.0 11.6 %copy-start.130 = (f32[2]{0:T(128)S(1)}, f32[2]{0:T(128)}, u32[]{:S(2)}) copy-start(f32[2]{0:T(128)} %copy-done.129) | copy-start | bytes 28
  28.0 11.6 %copy-start.134 = (f32[2]{0:T(128)S(1)}, f32[2]{0:T(128)}, u32[]{:S(2)}) copy-start(f32[2]{0:T(128)} %copy-done.133) | copy-start | bytes 28
  28.0 11.6 %copy-start.138 = (f32[2]{0:T(128)S(1)}, f32[2]{0:T(128)}, u32[]{:S(2)}) copy-start(f32[2]{0:T(128)} %copy-done.137) | copy-start | bytes 28
  30.5 121.8 %collective-permute-start.1 = (f32[1,2,1024]{2,1,0:T(2,128)}, f32[1,2,1024]{2,1,0:T(2,128)}, u32[]{:S(2)}, u32[]{:S(2)}) collective-permute-start(f32[1,2,1024]{2,1,0:T(2,128)} %stack_reshape_squeeze.37), channel_id=1, source_target_pairs={{0,1},{1,2},{2,3},{3,4},{4,5},{5,6},{6,7},{7,8},{8,9},{9,10},{10,1... | collective-permute-start | bytes 24584 | tf_op jit(solution)/shard_map/ppermute | solution.py:18
  36.1 115.4 %collective-permute-start = (f32[1,2,1024]{2,1,0:T(2,128)}, f32[1,2,1024]{2,1,0:T(2,128)}, u32[]{:S(2)}, u32[]{:S(2)}) collective-permute-start(f32[1,2,1024]{2,1,0:T(2,128)} %stack_reshape_squeeze.36), channel_id=1, source_target_pairs={{1,0},{2,1},{3,2},{4,3},{5,4},{6,5},{7,6},{8,7},{9,8},{10,9},{11,1... | collective-permute-start | bytes 24584 | tf_op jit(solution)/shard_map/ppermute | solution.py:21
  40.7 19.9 %copy-start.31 = (f32[2,32,1024]{2,1,0:T(8,128)}, f32[2,32,1024]{2,1,0:T(8,128)S(1)}, u32[]{:S(2)}) copy-start(f32[2,32,1024]{2,1,0:T(8,128)S(1)} %get-tuple-element.68) | copy-start | bytes 786436
  40.7 27.0 %copy-start.13 = (f32[2,32,1024]{2,1,0:T(8,128)}, f32[2,32,1024]{2,1,0:T(8,128)S(1)}, u32[]{:S(2)}) copy-start(f32[2,32,1024]{2,1,0:T(8,128)S(1)} %get-tuple-element.73) | copy-start | bytes 786436
  40.7 446.4 %copy-start.11 = (f32[2,32,1024]{2,1,0:T(8,128)}, f32[2,32,1024]{2,1,0:T(8,128)S(1)}, u32[]{:S(2)}) copy-start(f32[2,32,1024]{2,1,0:T(8,128)S(1)} %get-tuple-element.72) | copy-start | bytes 786436
  44.2 16.4 %copy-start.141 = (pred[8,4]{1,0:T(8,128)(4,1)}, pred[8,4]{1,0:T(8,128)(4,1)S(1)}, u32[]{:S(2)}) copy-start(pred[8,4]{1,0:T(8,128)(4,1)S(1)} %iota_compare_fusion.11) | copy-start | bytes 100
  68.2 21.3 %copy-start.7 = (f32[2,32,32,32]{3,2,1,0:T(8,128)S(1)}, f32[2,32,32,32]{3,2,1,0:T(8,128)}, u32[]{:S(2)}) copy-start(f32[2,32,32,32]{3,2,1,0:T(8,128)} %copy-done.6) | copy-start | bytes 786436
  89.5 47.8 %copy-start.59 = (f32[2,32,992]{2,1,0:T(8,128)S(1)}, f32[2,32,992]{2,1,0:T(8,128)}, u32[]{:S(2)}) copy-start(f32[2,32,992]{2,1,0:T(8,128)} %get-tuple-element.146) | copy-start | bytes 761860
  91.3 53.5 %copy-start.96 = (pred[32]{0:T(512)(128)(4,1)S(1)}, pred[32]{0:T(512)(128)(4,1)}, u32[]{:S(2)}) copy-start(pred[32]{0:T(512)(128)(4,1)} %copy-done.95) | copy-start | bytes 100
  91.3 54.2 %copy-start.102 = (pred[32]{0:T(512)(128)(4,1)S(1)}, pred[32]{0:T(512)(128)(4,1)}, u32[]{:S(2)}) copy-start(pred[32]{0:T(512)(128)(4,1)} %copy-done.101) | copy-start | bytes 100
  126.0 22.8 %copy-start.81 = (f32[2,32,32]{2,1,0:T(8,128)}, f32[2,32,32]{2,1,0:T(8,128)S(1)}, u32[]{:S(2)}) copy-start(f32[2,32,32]{2,1,0:T(8,128)S(1)} %reshape.2206) | copy-start | bytes 24580
  126.8 22.1 %copy-start.82 = (f32[2,32,32]{2,1,0:T(8,128)}, f32[2,32,32]{2,1,0:T(8,128)S(1)}, u32[]{:S(2)}) copy-start(f32[2,32,32]{2,1,0:T(8,128)S(1)} %reshape.2205) | copy-start | bytes 24580
  137.4 11.5 %copy-start.57 = (f32[2,31,1024]{2,1,0:T(8,128)S(1)}, f32[2,31,1024]{2,1,0:T(8,128)}, u32[]{:S(2)}) copy-start(f32[2,31,1024]{2,1,0:T(8,128)} %get-tuple-element.142) | copy-start | bytes 761860
  138.6 14.4 %copy-start.156 = (f32[2]{0:T(128)}, f32[2]{0:T(128)S(1)}, u32[]{:S(2)}) copy-start(f32[2]{0:T(128)S(1)} %fusion.180) | copy-start | bytes 28
  221.3 44.6 %collective-permute-start.3 = (f32[1,2,1024]{2,1,0:T(2,128)}, f32[1,2,1024]{2,1,0:T(2,128)}, u32[]{:S(2)}, u32[]{:S(2)}) collective-permute-start(f32[1,2,1024]{2,1,0:T(2,128)} %stack_reshape_squeeze.39), channel_id=1, source_target_pairs={{0,1},{1,2},{2,3},{3,4},{4,5},{5,6},{6,7},{7,8},{8,9},{9,10},{10,1... | collective-permute-start | bytes 24584 | tf_op jit(solution)/shard_map/ppermute | solution.py:18
  223.2 51.0 %collective-permute-start.2 = (f32[1,2,1024]{2,1,0:T(2,128)}, f32[1,2,1024]{2,1,0:T(2,128)}, u32[]{:S(2)}, u32[]{:S(2)}) collective-permute-start(f32[1,2,1024]{2,1,0:T(2,128)} %stack_reshape_squeeze.38), channel_id=1, source_target_pairs={{1,0},{2,1},{3,2},{4,3},{5,4},{6,5},{7,6},{8,7},{9,8},{10,9},{11,1... | collective-permute-start | bytes 24584 | tf_op jit(solution)/shard_map/ppermute | solution.py:21
  359.8 19.8 %copy-start.34 = (f32[2,32,1024]{2,1,0:T(8,128)S(1)}, f32[2,32,1024]{2,1,0:T(8,128)}, u32[]{:S(2)}) copy-start(f32[2,32,1024]{2,1,0:T(8,128)} %copy-done.33) | copy-start | bytes 786436
  436.2 39.2 %collective-permute-start.5 = (f32[1,2,1024]{2,1,0:T(2,128)}, f32[1,2,1024]{2,1,0:T(2,128)}, u32[]{:S(2)}, u32[]{:S(2)}) collective-permute-start(f32[1,2,1024]{2,1,0:T(2,128)} %stack_reshape_squeeze.41), channel_id=1, source_target_pairs={{0,1},{1,2},{2,3},{3,4},{4,5},{5,6},{6,7},{7,8},{8,9},{9,10},{10,1... | collective-permute-start | bytes 24584 | tf_op jit(solution)/shard_map/ppermute | solution.py:18
  438.1 43.2 %collective-permute-start.4 = (f32[1,2,1024]{2,1,0:T(2,128)}, f32[1,2,1024]{2,1,0:T(2,128)}, u32[]{:S(2)}, u32[]{:S(2)}) collective-permute-start(f32[1,2,1024]{2,1,0:T(2,128)} %stack_reshape_squeeze.40), channel_id=1, source_target_pairs={{1,0},{2,1},{3,2},{4,3},{5,4},{6,5},{7,6},{8,7},{9,8},{10,9},{11,1... | collective-permute-start | bytes 24584 | tf_op jit(solution)/shard_map/ppermute | solution.py:21
  599.9 27.8 %collective-permute-start.7 = (f32[1,2,1024]{2,1,0:T(2,128)}, f32[1,2,1024]{2,1,0:T(2,128)}, u32[]{:S(2)}, u32[]{:S(2)}) collective-permute-start(f32[1,2,1024]{2,1,0:T(2,128)} %stack_reshape_squeeze.43), channel_id=1, source_target_pairs={{0,1},{1,2},{2,3},{3,4},{4,5},{5,6},{6,7},{7,8},{8,9},{9,10},{10,1... | collective-permute-start | bytes 24584 | tf_op jit(solution)/shard_map/ppermute | solution.py:18
  602.1 30.7 %collective-permute-start.6 = (f32[1,2,1024]{2,1,0:T(2,128)}, f32[1,2,1024]{2,1,0:T(2,128)}, u32[]{:S(2)}, u32[]{:S(2)}) collective-permute-start(f32[1,2,1024]{2,1,0:T(2,128)} %stack_reshape_squeeze.42), channel_id=1, source_target_pairs={{1,0},{2,1},{3,2},{4,3},{5,4},{6,5},{7,6},{8,7},{9,8},{10,9},{11,1... | collective-permute-start | bytes 24584 | tf_op jit(solution)/shard_map/ppermute | solution.py:21
  607.5 10.3 copy-start.22
  637.4 70.8 %copy-start.45 = (f32[2,32,1024]{2,1,0:T(8,128)S(1)}, f32[2,32,1024]{2,1,0:T(8,128)}, u32[]{:S(2)}) copy-start(f32[2,32,1024]{2,1,0:T(8,128)} %copy-done.44) | copy-start | bytes 786436
  709.7 18.3 %copy-start.54 = (f32[2,32,1024]{2,1,0:T(8,128)}, f32[2,32,1024]{2,1,0:T(8,128)S(1)}, u32[]{:S(2)}) copy-start(f32[2,32,1024]{2,1,0:T(8,128)S(1)} %get-tuple-element.47) | copy-start | bytes 786436
  783.5 36.6 %collective-permute-start.9 = (f32[1,2,1024]{2,1,0:T(2,128)}, f32[1,2,1024]{2,1,0:T(2,128)}, u32[]{:S(2)}, u32[]{:S(2)}) collective-permute-start(f32[1,2,1024]{2,1,0:T(2,128)} %stack_reshape_squeeze.45), channel_id=1, source_target_pairs={{0,1},{1,2},{2,3},{3,4},{4,5},{5,6},{6,7},{7,8},{8,9},{9,10},{10,1... | collective-permute-start | bytes 24584 | tf_op jit(solution)/shard_map/ppermute | solution.py:18
  785.4 40.6 %collective-permute-start.8 = (f32[1,2,1024]{2,1,0:T(2,128)}, f32[1,2,1024]{2,1,0:T(2,128)}, u32[]{:S(2)}, u32[]{:S(2)}) collective-permute-start(f32[1,2,1024]{2,1,0:T(2,128)} %stack_reshape_squeeze.44), channel_id=1, source_target_pairs={{1,0},{2,1},{3,2},{4,3},{5,4},{6,5},{7,6},{8,7},{9,8},{10,9},{11,1... | collective-permute-start | bytes 24584 | tf_op jit(solution)/shard_map/ppermute | solution.py:21
  823.6 8.3 copy-start.108
  823.6 8.3 copy-start.110
  823.6 8.3 copy-start.120
  913.2 19.4 %copy-start.36 = (f32[2,32,1024]{2,1,0:T(8,128)S(1)}, f32[2,32,1024]{2,1,0:T(8,128)}, u32[]{:S(2)}) copy-start(f32[2,32,1024]{2,1,0:T(8,128)} %copy-done.35) | copy-start | bytes 786436
  952.7 22.7 %collective-permute-start.11 = (f32[1,2,1024]{2,1,0:T(2,128)S(1)}, f32[1,2,1024]{2,1,0:T(2,128)S(1)}, u32[]{:S(2)}, u32[]{:S(2)}) collective-permute-start(f32[1,2,1024]{2,1,0:T(2,128)S(1)} %stack_reshape_squeeze.47), channel_id=1, source_target_pairs={{0,1},{1,2},{2,3},{3,4},{4,5},{5,6},{6,7},{7,8},{8,9},{9,10},{10,1... | collective-permute-start | bytes 24584 | tf_op jit(solution)/shard_map/ppermute | solution.py:18
  954.2 26.3 %collective-permute-start.10 = (f32[1,2,1024]{2,1,0:T(2,128)S(1)}, f32[1,2,1024]{2,1,0:T(2,128)S(1)}, u32[]{:S(2)}, u32[]{:S(2)}) collective-permute-start(f32[1,2,1024]{2,1,0:T(2,128)S(1)} %stack_reshape_squeeze.46), channel_id=1, source_target_pairs={{1,0},{2,1},{3,2},{4,3},{5,4},{6,5},{7,6},{8,7},{9,8},{10,9},{11,1... | collective-permute-start | bytes 24584 | tf_op jit(solution)/shard_map/ppermute | solution.py:21
  984.3 72.3 %copy-start.40 = (f32[1,1,2,32,1024]{4,3,2,1,0:T(8,128)S(1)}, f32[1,1,2,32,1024]{4,3,2,1,0:T(8,128)}, u32[]{:S(2)}) copy-start(f32[1,1,2,32,1024]{4,3,2,1,0:T(8,128)} %param.10) | copy-start | bytes 786436
  984.3 72.3 %copy-start.75 = (pred[32,1024]{1,0:T(8,128)(4,1)S(1)}, pred[32,1024]{1,0:T(8,128)(4,1)}, u32[]{:S(2)}) copy-start(pred[32,1024]{1,0:T(8,128)(4,1)} %copy-done.73) | copy-start | bytes 98308
  984.3 72.3 %copy-start.78 = (pred[32,1024]{1,0:T(8,128)(4,1)S(1)}, pred[32,1024]{1,0:T(8,128)(4,1)}, u32[]{:S(2)}) copy-start(pred[32,1024]{1,0:T(8,128)(4,1)} %copy-done.76) | copy-start | bytes 98308
  (131 other events, 441.1 us)
where the time goes:
time: 1080 us; the launch traced here: 1060 us
  blocking collectives  547 us (51%)
  local copies, waits for them, and re-layouts  336 us (31%)
  other arithmetic  139 us (13%)
  starting transfers between devices  22.6 us (2%)
  between operations  15.9 us (1%)
    psum x5, blocking collectives, global_sum(): return lax.psum(jnp.sum(values), ('brick', 'grp'))  339 us
    another operation x3, blocking collectives, coarse_solve(): lax.linalg.triangular_solve(factor, gathered_terms, left_side=True, lower...  94.1 us
    all_gather x6, blocking collectives, apply_operator(): portion = lax.all_gather(outgoing_sides[None], 'brick', axis=0, tiled=True)  94.1 us
    broadcast_in_dim x26, local copies, waits for them, and re-layouts, apply_operator(): jnp.where(cube_third == BS - 1, from_above, jnp.roll(cube, -1, axis=3))  45 us
    broadcast_in_dim x26, local copies, waits for them, and re-layouts, apply_operator(): jnp.where(cube_third == 0, from_below, jnp.roll(cube, 1, axis=3))  43.7 us
    concatenate x12, local copies, waits for them, and re-layouts, apply_operator(): jnp.roll(cube, -1, axis=3)  26.6 us
    concatenate x12, local copies, waits for them, and re-layouts, apply_operator(): jnp.roll(cube, 1, axis=3)  25.4 us
    div x6, other arithmetic, precondition(): smoothed = OMEGA * residual_field / diagonal  24.1 us
  transfers between devices with their start and end apart: 12, of which 0 were waited for; matrix products, arithmetic and copies ran while one was open for 21% of the time, Pallas kernels for 0%

commit v1 on v0

--- a/solution.py
+++ b/solution.py
@@ -119,7 +119,12 @@
                 pad_rows(grid_upper_y[:, PATCH_Y - 1], capacity),
             ]
         )
-        portion = lax.all_gather(outgoing_sides[None], "brick", axis=0, tiled=True)
+        portion = jnp.concatenate(
+            lax.all_to_all(
+                jnp.stack([outgoing_sides[None]] * lax.axis_size("brick")), "brick", 0, 0
+            ),
+            axis=0,
+        )
         sources = jnp.arange(portion.shape[0], dtype=jnp.int32)
         matches = sources[:, None] == wanted[None, :]
         remote = jnp.zeros((4, capacity, face_size), jnp.float32) + jnp.sum(

time: 1080 us -> 1050 us (0.972)
  blocking collectives: 547 us -> 441 us
  starting transfers between devices: 22.6 us -> 84.3 us
  other arithmetic: 139 us -> 150 us
    all_gather x6 -> x0, blocking collectives: 94.1 us -> none  [apply_operator(): portion = lax.all_gather(outgoing_sides[None], 'brick', axis=0, tiled=True)]
    all_to_all x0 -> x6, starting transfers between devices: none -> 56.6 us  [apply_operator(): lax.all_to_all(jnp.stack([outgoing_sides[None]] * lax.axis_size('brick'))...]
    psum x5, blocking collectives: 339 us -> 327 us  [global_sum(): return lax.psum(jnp.sum(values), ('brick', 'grp'))]
    another operation x3 -> x22, local copies, waits for them, and re-layouts: 1.1 us -> 12.7 us  [the longest x6 4.73 us: apply_operator(): jnp.stack([outgoing_sides[None]] * lax.axis_size('brick'))]
    unnamed x350 -> x328, local copies, waits for them, and re-layouts: 19.7 us -> 8.4 us
    concatenate x14 -> x24, local copies, waits for them, and re-layouts: 20.9 us -> 29.6 us  [apply_operator(): jnp.concatenate([field[:, 1:, :], beyond_xplus[:, None, :]], axis=1)]
  transfers between devices with their start and end apart: 12 -> 18, of which waited for: 0 -> 0; matrix products, arithmetic and copies ran while one was open for 21% -> 25% of each run, Pallas kernels for 0% -> 0%
where the time goes in v1:
time: 1050 us; the launch traced here: 1030 us
  blocking collectives  441 us (42%)
  local copies, waits for them, and re-layouts  339 us (32%)
  other arithmetic  150 us (14%)
  starting transfers between devices  84.3 us (8%)
  between operations  15 us (1%)
    psum x5, blocking collectives, global_sum(): return lax.psum(jnp.sum(values), ('brick', 'grp'))  327 us
    another operation x3, blocking collectives, coarse_solve(): lax.linalg.triangular_solve(factor, gathered_terms, left_side=True, lower...  94.1 us
    all_to_all x6, starting transfers between devices, apply_operator(): lax.all_to_all(jnp.stack([outgoing_sides[None]] * lax.axis_size('brick'))...  56.6 us
    broadcast_in_dim x26, local copies, waits for them, and re-layouts, apply_operator(): jnp.where(cube_third == BS - 1, from_above, jnp.roll(cube, -1, axis=3))  43 us
    broadcast_in_dim x26, local copies, waits for them, and re-layouts, apply_operator(): jnp.where(cube_third == 0, from_below, jnp.roll(cube, 1, axis=3))  36 us
    concatenate x24, local copies, waits for them, and re-layouts, apply_operator(): jnp.concatenate([field[:, 1:, :], beyond_xplus[:, None, :]], axis=1)  29.6 us
    concatenate x12, local copies, waits for them, and re-layouts, apply_operator(): jnp.roll(cube, -1, axis=3)  26.6 us
    div x6, other arithmetic, precondition(): smoothed = OMEGA * residual_field / diagonal  25.5 us
  transfers between devices with their start and end apart: 18, of which 0 were waited for; matrix products, arithmetic and copies ran while one was open for 25% of the time, Pallas kernels for 0%

profile of v1, /device:TPU:1, one launch (start us, length us, event | category | flops | bytes accessed | tf_op | source)
XLA Modules:
  0.0 1031.8 jit_solution(8979715707319562568)
XLA Ops:
  6.4 2.6 multiply_divide_fusion.5
  11.5 6.1 all-to-all-start
  27.6 2.4 squeeze.120
  38.6 5.7 multiply_divide_fusion.2
  46.8 4.1 collective-permute-start.1
  63.4 19.9 %all-gather.4 = f32[16,4,2]{1,2,0:T(2,128)S(1)} all-gather(f32[1,4,2]{1,2,0:T(2,128)S(1)} %bitcast.582), channel_id=2, replica_groups=mesh['brick'=8,'grp'=16] {'grp'}, dimensions={0}, use_global_device_ids=true | all-gather | bytes 544 | tf_op jit(solution)/shard_map/all_gather | solution.py:194
  88.8 31.0 %all-reduce.18 = f32[32]{0:T(128)S(1)} all-reduce(f32[32]{0:T(128)S(1)} %dynamic-update-slice.3), channel_id=3, replica_groups=mesh['brick'=8,'grp'=16] {'grp'}, use_global_device_ids=true, to_apply=%add.18 | all-reduce | flops 32 | bytes 256 | tf_op jit(solution)/shard_map/triangular_solve/reshape.99 | solution.py:202
  123.3 2.9 cholesky.19
  127.5 2.4 custom-call.14
  158.8 8.4 fusion.46
  167.2 2.4 concatenate.643
  189.7 17.8 %all-to-all-start.1 = ((f32[8,1,4,2,1024]{4,3,2,1,0:T(2,128)}), f32[8,1,4,2,1024]{4,3,2,1,0:T(2,128)}, u32[]{:S(2)}, u32[]{:S(2)}) async-start(f32[8,1,4,2,1024]{4,3,2,1,0:T(2,128)} %stack.147), calls=%async_computation.1 | async-start | bytes 524288 | tf_op jit(solution)/shard_map/all_to_all | solution.py:123
  213.7 3.0 pad_maximum_fusion.2
  220.9 2.4 concatenate.676
  233.0 2.4 concatenate.663
  271.1 3.9 multiply_reduce_fusion.3
  274.9 64.7 %all-reduce.21 = (f32[]{:T(128)}, f32[]{:T(128)}) all-reduce(f32[]{:T(128)} %get-tuple-element.17, f32[]{:T(128)} %get-tuple-element.16), channel_id=1, replica_groups=mesh['brick'=8,'grp'=16] {'brick','grp'}, use_global_device_ids=true, to_apply=%region_16.19 | all-reduce | flops 2 | bytes 16 | tf_op jit(solution)/shard_map/psum | solution.py:218
  353.6 8.9 multiply_divide_fusion.1
  369.6 31.3 %all-reduce.19 = f32[32]{0:T(128)} all-reduce(f32[32]{0:T(128)} %dynamic-update-slice.4), channel_id=4, replica_groups=mesh['brick'=8,'grp'=16] {'grp'}, use_global_device_ids=true, to_apply=%add.19 | all-reduce | flops 32 | bytes 256 | tf_op jit(solution)/shard_map/triangular_solve/reshape.99 | solution.py:202
  410.2 11.8 %all-to-all-start.2 = ((f32[8,1,4,2,1024]{4,3,2,1,0:T(2,128)}), f32[8,1,4,2,1024]{4,3,2,1,0:T(2,128)}, u32[]{:S(2)}, u32[]{:S(2)}) async-start(f32[8,1,4,2,1024]{4,3,2,1,0:T(2,128)} %stack.153), calls=%async_computation.2 | async-start | bytes 524288 | tf_op jit(solution)/shard_map/all_to_all | solution.py:123
  428.9 3.1 pad_maximum_fusion.4
  432.2 3.4 fusion.96
  444.8 2.4 concatenate.695
  477.4 3.8 multiply_reduce_fusion.2
  481.1 64.5 %psum.44 = f32[]{:T(128)} all-reduce(f32[]{:T(128)} %get-tuple-element.50), channel_id=1, replica_groups=mesh['brick'=8,'grp'=16] {'brick','grp'}, use_global_device_ids=true, to_apply=%region_23.26 | all-reduce | flops 1 | bytes 8 | tf_op jit(solution)/shard_map/psum | solution.py:218
  558.4 7.2 multiply_add_fusion.1
  571.3 4.6 all-to-all-start.3
  577.2 4.8 collective-permute-start.7
  583.5 2.7 pad_maximum_fusion.6
  591.4 2.5 concatenate.791
  607.5 2.5 broadcast_in_dim.756
  616.9 3.4 multiply_reduce_fusion.1
  620.3 66.2 %psum.45 = f32[]{:T(128)} all-reduce(f32[]{:T(128)} %get-tuple-element.46), channel_id=1, replica_groups=mesh['brick'=8,'grp'=16] {'brick','grp'}, use_global_device_ids=true, to_apply=%region_26.29 | all-reduce | flops 1 | bytes 8 | tf_op jit(solution)/shard_map/psum | solution.py:218
  701.1 8.2 multiply_divide_fusion
  715.1 31.7 %all-reduce.20 = f32[32]{0:T(128)} all-reduce(f32[32]{0:T(128)} %dynamic-update-slice.5), channel_id=5, replica_groups=mesh['brick'=8,'grp'=16] {'grp'}, use_global_device_ids=true, to_apply=%add.20 | all-reduce | flops 32 | bytes 256 | tf_op jit(solution)/shard_map/triangular_solve/reshape.99 | solution.py:202
  752.7 11.8 %all-to-all-start.4 = ((f32[8,1,4,2,1024]{4,3,2,1,0:T(2,128)}), f32[8,1,4,2,1024]{4,3,2,1,0:T(2,128)}, u32[]{:S(2)}, u32[]{:S(2)}) async-start(f32[8,1,4,2,1024]{4,3,2,1,0:T(2,128)} %stack.165), calls=%async_computation.4 | async-start | bytes 524288 | tf_op jit(solution)/shard_map/all_to_all | solution.py:123
  770.5 3.0 pad_maximum_fusion.8
  781.7 2.4 concatenate.805
  806.6 2.4 broadcast_in_dim.745
  818.0 3.8 multiply_reduce_fusion
  821.7 64.4 %psum.46 = f32[]{:T(128)} all-reduce(f32[]{:T(128)} %get-tuple-element.38), channel_id=1, replica_groups=mesh['brick'=8,'grp'=16] {'brick','grp'}, use_global_device_ids=true, to_apply=%region_30.33 | all-reduce | flops 1 | bytes 8 | tf_op jit(solution)/shard_map/psum | solution.py:218
  899.1 10.7 %multiply_add_fusion = f32[2,32,32,32]{3,2,1,0:T(8,128)S(1)} fusion(f32[2,32,32,32]{3,2,1,0:T(8,128)} %copy-done.5, f32[2,32,32,32]{3,2,1,0:T(8,128)} %get-tuple-element.71, f32[2,32,32,32]{3,2,1,0:T(8,128)} %get-tuple-element.73, f32[2,32,32,32]{3,2,1,0:T(8,128)} %get-tuple-element.72, f32[2,32,32,32]{3,2,1,0:T(8,128)} %concatenate.773, ...), kind=kLoop, calls=%fused_computation.76 | loop fusion | flops 3735552 | bytes 5865592 | tf_op jit(solution)/shard_map/add | solution.py:230
  915.8 4.6 all-to-all-start.5
  920.5 4.4 collective-permute-start.11
  944.0 2.5 broadcast_in_dim.760
  954.1 2.6 fusion.161
  956.8 66.7 %psum.47 = f32[]{:T(128)} all-reduce(f32[]{:T(128)} %fusion.161), channel_id=1, replica_groups=mesh['brick'=8,'grp'=16] {'brick','grp'}, use_global_device_ids=true, to_apply=%region_33.36 | all-reduce | flops 1 | bytes 8 | tf_op jit(solution)/shard_map/psum | solution.py:218
  1024.8 6.0 fusion.149
  (730 shorter events, 386.0 us)
Async XLA Ops:
  4.5 34.1 %copy-start.93 = (pred[32]{0:T(512)(128)(4,1)}, pred[32]{0:T(512)(128)(4,1)S(1)}, u32[]{:S(2)}) copy-start(pred[32]{0:T(512)(128)(4,1)S(1)} %iota_compare_fusion.13) | copy-start | bytes 100
  4.5 34.1 %copy-start.98 = (pred[32]{0:T(512)(128)(4,1)}, pred[32]{0:T(512)(128)(4,1)S(1)}, u32[]{:S(2)}) copy-start(pred[32]{0:T(512)(128)(4,1)S(1)} %iota_compare_fusion.12) | copy-start | bytes 100
  5.7 48.4 %copy-start.79 = (f32[2]{0:T(128)}, f32[2]{0:T(128)S(1)}, u32[]{:S(2)}) copy-start(f32[2]{0:T(128)S(1)} %get-tuple-element.28) | copy-start | bytes 28
  5.9 32.7 %copy-start.117 = (f32[2]{0:T(128)}, f32[2]{0:T(128)S(1)}, u32[]{:S(2)}) copy-start(f32[2]{0:T(128)S(1)} %get-tuple-element.262) | copy-start | bytes 28
  6.4 14.8 %copy-start.20 = (f32[1,1,2,32,1024]{4,3,2,1,0:T(8,128)S(1)}, f32[1,1,2,32,1024]{4,3,2,1,0:T(8,128)}, u32[]{:S(2)}) copy-start(f32[1,1,2,32,1024]{4,3,2,1,0:T(8,128)} %param.9) | copy-start | bytes 786436
  9.1 14.8 %copy-start.31 = (f32[2,32,1024]{2,1,0:T(8,128)}, f32[2,32,1024]{2,1,0:T(8,128)S(1)}, u32[]{:S(2)}) copy-start(f32[2,32,1024]{2,1,0:T(8,128)S(1)} %get-tuple-element.64) | copy-start | bytes 786436
  9.1 53.4 %copy-start.13 = (f32[2,32,1024]{2,1,0:T(8,128)}, f32[2,32,1024]{2,1,0:T(8,128)S(1)}, u32[]{:S(2)}) copy-start(f32[2,32,1024]{2,1,0:T(8,128)S(1)} %get-tuple-element.69) | copy-start | bytes 786436
  9.1 468.3 %copy-start.11 = (f32[2,32,1024]{2,1,0:T(8,128)}, f32[2,32,1024]{2,1,0:T(8,128)S(1)}, u32[]{:S(2)}) copy-start(f32[2,32,1024]{2,1,0:T(8,128)S(1)} %get-tuple-element.68) | copy-start | bytes 786436
  9.1 13.5 %copy-start.32 = (f32[1,1,2,32,1024]{4,3,2,1,0:T(8,128)S(1)}, f32[1,1,2,32,1024]{4,3,2,1,0:T(8,128)}, u32[]{:S(2)}) copy-start(f32[1,1,2,32,1024]{4,3,2,1,0:T(8,128)} %param.10) | copy-start | bytes 786436
  11.5 12.4 %copy-start = (f32[1,1,6,2,32,1024]{5,4,3,2,1,0:T(8,128)S(1)}, f32[1,1,6,2,32,1024]{5,4,3,2,1,0:T(8,128)}, u32[]{:S(2)}) copy-start(f32[1,1,6,2,32,1024]{5,4,3,2,1,0:T(8,128)} %param.11) | copy-start | bytes 4718596
  11.5 136.8 %all-to-all-start = ((f32[8,1,4,2,1024]{4,3,2,1,0:T(2,128)}), f32[8,1,4,2,1024]{4,3,2,1,0:T(2,128)}, u32[]{:S(2)}, u32[]{:S(2)}) async-start(f32[8,1,4,2,1024]{4,3,2,1,0:T(2,128)} %stack.140), calls=%async_computation | async-start | bytes 524288 | tf_op jit(solution)/shard_map/all_to_all | solution.py:123
  27.6 11.0 %copy-start.1 = (f32[2,32,32,32]{3,2,1,0:T(8,128)}, f32[2,32,32,32]{3,2,1,0:T(8,128)S(1)}, u32[]{:S(2)}) copy-start(f32[2,32,32,32]{3,2,1,0:T(8,128)S(1)} %squeeze.121) | copy-start | bytes 786436
  44.3 9.8 copy-start.21
  46.8 97.4 %collective-permute-start.1 = (f32[1,2,1024]{2,1,0:T(2,128)}, f32[1,2,1024]{2,1,0:T(2,128)}, u32[]{:S(2)}, u32[]{:S(2)}) collective-permute-start(f32[1,2,1024]{2,1,0:T(2,128)} %stack_reshape_squeeze.37), channel_id=1, source_target_pairs={{0,1},{1,2},{2,3},{3,4},{4,5},{5,6},{6,7},{7,8},{8,9},{9,10},{10,1... | collective-permute-start | bytes 24584 | tf_op jit(solution)/shard_map/ppermute | solution.py:18
  51.6 89.0 %collective-permute-start = (f32[1,2,1024]{2,1,0:T(2,128)}, f32[1,2,1024]{2,1,0:T(2,128)}, u32[]{:S(2)}, u32[]{:S(2)}) collective-permute-start(f32[1,2,1024]{2,1,0:T(2,128)} %stack_reshape_squeeze.36), channel_id=1, source_target_pairs={{1,0},{2,1},{3,2},{4,3},{5,4},{6,5},{7,6},{8,7},{9,8},{10,9},{11,1... | collective-permute-start | bytes 24584 | tf_op jit(solution)/shard_map/ppermute | solution.py:21
  63.0 21.3 %copy-start.7 = (f32[2,32,32,32]{3,2,1,0:T(8,128)S(1)}, f32[2,32,32,32]{3,2,1,0:T(8,128)}, u32[]{:S(2)}) copy-start(f32[2,32,32,32]{3,2,1,0:T(8,128)} %copy-done.6) | copy-start | bytes 786436
  84.3 53.7 %copy-start.53 = (f32[2,31,1024]{2,1,0:T(8,128)S(1)}, f32[2,31,1024]{2,1,0:T(8,128)}, u32[]{:S(2)}) copy-start(f32[2,31,1024]{2,1,0:T(8,128)} %get-tuple-element.138) | copy-start | bytes 761860
  86.0 53.3 %copy-start.54 = (f32[2,31,1024]{2,1,0:T(8,128)S(1)}, f32[2,31,1024]{2,1,0:T(8,128)}, u32[]{:S(2)}) copy-start(f32[2,31,1024]{2,1,0:T(8,128)} %get-tuple-element.139) | copy-start | bytes 761860
  189.7 69.5 %all-to-all-start.1 = ((f32[8,1,4,2,1024]{4,3,2,1,0:T(2,128)}), f32[8,1,4,2,1024]{4,3,2,1,0:T(2,128)}, u32[]{:S(2)}, u32[]{:S(2)}) async-start(f32[8,1,4,2,1024]{4,3,2,1,0:T(2,128)} %stack.147), calls=%async_computation.1 | async-start | bytes 524288 | tf_op jit(solution)/shard_map/all_to_all | solution.py:123
  210.4 32.2 %collective-permute-start.3 = (f32[1,2,1024]{2,1,0:T(2,128)}, f32[1,2,1024]{2,1,0:T(2,128)}, u32[]{:S(2)}, u32[]{:S(2)}) collective-permute-start(f32[1,2,1024]{2,1,0:T(2,128)} %stack_reshape_squeeze.39), channel_id=1, source_target_pairs={{0,1},{1,2},{2,3},{3,4},{4,5},{5,6},{6,7},{7,8},{8,9},{9,10},{10,1... | collective-permute-start | bytes 24584 | tf_op jit(solution)/shard_map/ppermute | solution.py:18
  212.2 38.7 %collective-permute-start.2 = (f32[1,2,1024]{2,1,0:T(2,128)}, f32[1,2,1024]{2,1,0:T(2,128)}, u32[]{:S(2)}, u32[]{:S(2)}) collective-permute-start(f32[1,2,1024]{2,1,0:T(2,128)} %stack_reshape_squeeze.38), channel_id=1, source_target_pairs={{1,0},{2,1},{3,2},{4,3},{5,4},{6,5},{7,6},{8,7},{9,8},{10,9},{11,1... | collective-permute-start | bytes 24584 | tf_op jit(solution)/shard_map/ppermute | solution.py:21
  410.2 58.2 %all-to-all-start.2 = ((f32[8,1,4,2,1024]{4,3,2,1,0:T(2,128)}), f32[8,1,4,2,1024]{4,3,2,1,0:T(2,128)}, u32[]{:S(2)}, u32[]{:S(2)}) async-start(f32[8,1,4,2,1024]{4,3,2,1,0:T(2,128)} %stack.153), calls=%async_computation.2 | async-start | bytes 524288 | tf_op jit(solution)/shard_map/all_to_all | solution.py:123
  424.9 26.9 %collective-permute-start.5 = (f32[1,2,1024]{2,1,0:T(2,128)}, f32[1,2,1024]{2,1,0:T(2,128)}, u32[]{:S(2)}, u32[]{:S(2)}) collective-permute-start(f32[1,2,1024]{2,1,0:T(2,128)} %stack_reshape_squeeze.41), channel_id=1, source_target_pairs={{0,1},{1,2},{2,3},{3,4},{4,5},{5,6},{6,7},{7,8},{8,9},{9,10},{10,1... | collective-permute-start | bytes 24584 | tf_op jit(solution)/shard_map/ppermute | solution.py:18
  426.8 33.3 %collective-permute-start.4 = (f32[1,2,1024]{2,1,0:T(2,128)}, f32[1,2,1024]{2,1,0:T(2,128)}, u32[]{:S(2)}, u32[]{:S(2)}) collective-permute-start(f32[1,2,1024]{2,1,0:T(2,128)} %stack_reshape_squeeze.40), channel_id=1, source_target_pairs={{1,0},{2,1},{3,2},{4,3},{5,4},{6,5},{7,6},{8,7},{9,8},{10,9},{11,1... | collective-permute-start | bytes 24584 | tf_op jit(solution)/shard_map/ppermute | solution.py:21
  567.2 16.4 %copy-start.8 = (f32[2,32,32,31]{3,2,1,0:T(8,128)}, f32[2,32,32,31]{3,2,1,0:T(8,128)S(1)}, u32[]{:S(2)}) copy-start(f32[2,32,32,31]{3,2,1,0:T(8,128)S(1)} %get-tuple-element.88) | copy-start | bytes 761860
  571.3 41.1 %all-to-all-start.3 = ((f32[8,1,4,2,1024]{4,3,2,1,0:T(2,128)}), f32[8,1,4,2,1024]{4,3,2,1,0:T(2,128)}, u32[]{:S(2)}, u32[]{:S(2)}) async-start(f32[8,1,4,2,1024]{4,3,2,1,0:T(2,128)} %stack.159), calls=%async_computation.3 | async-start | bytes 524288 | tf_op jit(solution)/shard_map/all_to_all | solution.py:123
  577.2 24.0 %collective-permute-start.7 = (f32[1,2,1024]{2,1,0:T(2,128)}, f32[1,2,1024]{2,1,0:T(2,128)}, u32[]{:S(2)}, u32[]{:S(2)}) collective-permute-start(f32[1,2,1024]{2,1,0:T(2,128)} %stack_reshape_squeeze.43), channel_id=1, source_target_pairs={{0,1},{1,2},{2,3},{3,4},{4,5},{5,6},{6,7},{7,8},{8,9},{9,10},{10,1... | collective-permute-start | bytes 24584 | tf_op jit(solution)/shard_map/ppermute | solution.py:18
  582.0 22.8 %collective-permute-start.6 = (f32[1,2,1024]{2,1,0:T(2,128)}, f32[1,2,1024]{2,1,0:T(2,128)}, u32[]{:S(2)}, u32[]{:S(2)}) collective-permute-start(f32[1,2,1024]{2,1,0:T(2,128)} %stack_reshape_squeeze.42), channel_id=1, source_target_pairs={{1,0},{2,1},{3,2},{4,3},{5,4},{6,5},{7,6},{8,7},{9,8},{10,9},{11,1... | collective-permute-start | bytes 24584 | tf_op jit(solution)/shard_map/ppermute | solution.py:21
  607.5 9.4 copy-start.12
  616.9 70.9 %copy-start.39 = (f32[2,32,1024]{2,1,0:T(8,128)S(1)}, f32[2,32,1024]{2,1,0:T(8,128)}, u32[]{:S(2)}) copy-start(f32[2,32,1024]{2,1,0:T(8,128)} %copy-done.38) | copy-start | bytes 786436
  752.7 56.4 %all-to-all-start.4 = ((f32[8,1,4,2,1024]{4,3,2,1,0:T(2,128)}), f32[8,1,4,2,1024]{4,3,2,1,0:T(2,128)}, u32[]{:S(2)}, u32[]{:S(2)}) async-start(f32[8,1,4,2,1024]{4,3,2,1,0:T(2,128)} %stack.165), calls=%async_computation.4 | async-start | bytes 524288 | tf_op jit(solution)/shard_map/all_to_all | solution.py:123
  767.4 25.1 %collective-permute-start.9 = (f32[1,2,1024]{2,1,0:T(2,128)}, f32[1,2,1024]{2,1,0:T(2,128)}, u32[]{:S(2)}, u32[]{:S(2)}) collective-permute-start(f32[1,2,1024]{2,1,0:T(2,128)} %stack_reshape_squeeze.45), channel_id=1, source_target_pairs={{0,1},{1,2},{2,3},{3,4},{4,5},{5,6},{6,7},{7,8},{8,9},{9,10},{10,1... | collective-permute-start | bytes 24584 | tf_op jit(solution)/shard_map/ppermute | solution.py:18
  769.2 31.5 %collective-permute-start.8 = (f32[1,2,1024]{2,1,0:T(2,128)}, f32[1,2,1024]{2,1,0:T(2,128)}, u32[]{:S(2)}, u32[]{:S(2)}) collective-permute-start(f32[1,2,1024]{2,1,0:T(2,128)} %stack_reshape_squeeze.44), channel_id=1, source_target_pairs={{1,0},{2,1},{3,2},{4,3},{5,4},{6,5},{7,6},{8,7},{9,8},{10,9},{11,1... | collective-permute-start | bytes 24584 | tf_op jit(solution)/shard_map/ppermute | solution.py:21
  804.2 13.8 %copy-start.83 = (f32[2]{0:T(128)S(1)}, f32[2]{0:T(128)}, u32[]{:S(2)}) copy-start(f32[2]{0:T(128)} %copy-done.79) | copy-start | bytes 28
  804.2 13.8 %copy-start.104 = (pred[1024]{0:T(1024)(128)(4,1)S(1)}, pred[1024]{0:T(1024)(128)(4,1)}, u32[]{:S(2)}) copy-start(pred[1024]{0:T(1024)(128)(4,1)} %broadcast_in_dim.679) | copy-start | bytes 3076
  804.2 13.8 %copy-start.106 = (pred[1024]{0:T(1024)(128)(4,1)S(1)}, pred[1024]{0:T(1024)(128)(4,1)}, u32[]{:S(2)}) copy-start(pred[1024]{0:T(1024)(128)(4,1)} %broadcast_in_dim.661) | copy-start | bytes 3076
  804.2 13.8 %copy-start.119 = (f32[2]{0:T(128)S(1)}, f32[2]{0:T(128)}, u32[]{:S(2)}) copy-start(f32[2]{0:T(128)} %copy-done.117) | copy-start | bytes 28
  915.8 33.1 %all-to-all-start.5 = ((f32[8,1,4,2,1024]{4,3,2,1,0:T(2,128)}), f32[8,1,4,2,1024]{4,3,2,1,0:T(2,128)}, u32[]{:S(2)}, u32[]{:S(2)}) async-start(f32[8,1,4,2,1024]{4,3,2,1,0:T(2,128)} %stack.171), calls=%async_computation.5 | async-start | bytes 524288 | tf_op jit(solution)/shard_map/all_to_all | solution.py:123
  920.5 19.2 %collective-permute-start.11 = (f32[1,2,1024]{2,1,0:T(2,128)S(1)}, f32[1,2,1024]{2,1,0:T(2,128)S(1)}, u32[]{:S(2)}, u32[]{:S(2)}) collective-permute-start(f32[1,2,1024]{2,1,0:T(2,128)S(1)} %stack_reshape_squeeze.47), channel_id=1, source_target_pairs={{0,1},{1,2},{2,3},{3,4},{4,5},{5,6},{6,7},{7,8},{8,9},{9,10},{10,1... | collective-permute-start | bytes 24584 | tf_op jit(solution)/shard_map/ppermute | solution.py:18
  924.9 17.6 %collective-permute-start.10 = (f32[1,2,1024]{2,1,0:T(2,128)S(1)}, f32[1,2,1024]{2,1,0:T(2,128)S(1)}, u32[]{:S(2)}, u32[]{:S(2)}) collective-permute-start(f32[1,2,1024]{2,1,0:T(2,128)S(1)} %stack_reshape_squeeze.46), channel_id=1, source_target_pairs={{1,0},{2,1},{3,2},{4,3},{5,4},{6,5},{7,6},{8,7},{9,8},{10,9},{11,1... | collective-permute-start | bytes 24584 | tf_op jit(solution)/shard_map/ppermute | solution.py:21
  943.9 10.1 copy-start.15
  943.9 10.1 copy-start.17
  943.9 10.1 copy-start.19
  944.0 10.1 copy-start.44
  944.0 10.1 copy-start.47
  954.1 70.6 %copy-start.34 = (f32[1,1,2,32,1024]{4,3,2,1,0:T(8,128)S(1)}, f32[1,1,2,32,1024]{4,3,2,1,0:T(8,128)}, u32[]{:S(2)}) copy-start(f32[1,1,2,32,1024]{4,3,2,1,0:T(8,128)} %param.10) | copy-start | bytes 786436
  954.1 70.6 %copy-start.67 = (pred[32,1024]{1,0:T(8,128)(4,1)S(1)}, pred[32,1024]{1,0:T(8,128)(4,1)}, u32[]{:S(2)}) copy-start(pred[32,1024]{1,0:T(8,128)(4,1)} %copy-done.65) | copy-start | bytes 98308
  954.1 70.6 %copy-start.70 = (pred[32,1024]{1,0:T(8,128)(4,1)S(1)}, pred[32,1024]{1,0:T(8,128)(4,1)}, u32[]{:S(2)}) copy-start(pred[32,1024]{1,0:T(8,128)(4,1)} %copy-done.68) | copy-start | bytes 98308
  (132 other events, 491.6 us)
